TPU v7x, 32 devices: a whole 2x2x4 slice. The times are simulated.
32 devices in a mesh: row: 4 (over y, core), col: 8 (over z, x).
Axes of the slice: x: 2, y: 2, z: 4, core: 2. Of those that a mesh axis runs over, the one named last changes fastest.
Arguments:
- elem_residual: bfloat16 [16384, 3, 256], P(('row', 'col')), may hold values from -6 to 6
- corners: int32 [16384, 3], P(('row', 'col')), may hold values from 0 to 383
- share_rows: int32 [32, 2, 64], P(('row', 'col')), may hold values from 0 to 255
- x_factor: bfloat16 [8192, 1728], P(('row', 'col')), may hold values from -0.40039062 to 0.40039062, as said below
Outputs:
- solution: float32 [8192, 256], P(('row', 'col'))
Inputs may be any that keep to these rules, and one draw needn't show every extreme that they name: `corners`: values below 256 are own vertices, the next 64 the slots shared with the left neighbour, the last 64 those shared with the right neighbour. `share_rows`: own row indices; a row may appear several times. `x_factor`: independent entries, each column block with its own scale.
All inputs are finite; a program needn't handle non-finite values.
Results may differ from a plain program's by a relative error of at most 0.0035.
Values sent between devices are 32-bit elements; how exact they have to be, the bound alone decides.
A program may use at most 64 MiB of HBM per device.

v0:
```python
import jax
import jax.numpy as jnp
from jax import lax
from jax.sharding import PartitionSpec as P

INNER = 1408
SEP_COLS = 64


def swapped(block, axis, stride):
    count = lax.axis_size(axis)
    route = []
    for low in range(count):
        high = low | 1 << stride
        if high != low and high < count:
            route += [(low, high), (high, low)]
    return lax.ppermute(block, axis, route)


def padded_2(block, sides, width):
    for axis, dim in sides:
        count = lax.axis_size(axis)
        forward = [(i, i + 1) for i in range(count - 1)]
        forward.append((count - 1, 0))
        backward = [(target, source) for source, target in forward]
        low = lax.ppermute(
            lax.slice_in_dim(block, block.shape[dim] - width, None, axis=dim), axis, forward
        )
        high = lax.ppermute(lax.slice_in_dim(block, 0, width, axis=dim), axis, backward)
        block = jnp.concatenate([low, block, high], axis=dim)
    return block


def col_rounds(blocks, count):
    col_bits = lax.axis_size("col").bit_length() - 1
    for bit in range(min(col_bits, count)):
        partner = swapped(blocks[bit:count], "col", bit)
        blocks = jnp.concatenate(
            [blocks[:bit], blocks[bit:count] + partner, blocks[count:]], axis=0
        )
    return blocks


def row_rounds(blocks, col_bits):
    row_bits = lax.axis_size("row").bit_length() - 1
    for bit in range(row_bits):
        start = col_bits + bit
        partner = swapped(blocks[start:], "row", bit)
        blocks = jnp.concatenate([blocks[:start], blocks[start:] + partner], axis=0)
    return blocks


def per_device(elem_residual, corners, share_rows, x_factor):
    rows_dev = x_factor.shape[0]
    shared = share_rows.shape[2]
    width = elem_residual.shape[2]
    ext_len = rows_dev + 2 * shared
    flat_ids = corners.reshape(-1)
    values = elem_residual.reshape(-1, width)
    onehot = (
        lax.broadcasted_iota(jnp.int32, (ext_len, flat_ids.shape[0]), 0) == flat_ids[None, :]
    ).astype(jnp.bfloat16)
    extended = jnp.dot(onehot, values, preferred_element_type=jnp.float32)
    padded = padded_2(extended[rows_dev:], (("col", 0),), shared)
    from_left = padded[:shared]
    from_right = padded[3 * shared :]
    row_ids = lax.broadcasted_iota(jnp.int32, (rows_dev, shared), 0)
    left_map = (row_ids == share_rows[0, 0][None, :]).astype(jnp.float32)
    right_map = (row_ids == share_rows[0, 1][None, :]).astype(jnp.float32)
    assembled = extended[:rows_dev]
    assembled = assembled + jnp.dot(
        left_map, from_left, precision=lax.Precision.HIGHEST, preferred_element_type=jnp.float32
    )
    assembled = assembled + jnp.dot(
        right_map, from_right, precision=lax.Precision.HIGHEST, preferred_element_type=jnp.float32
    )
    rhs_local = assembled.astype(jnp.bfloat16)
    partial_value = lax.dot_general(
        x_factor, rhs_local, (((0,), (0,)), ((), ())), preferred_element_type=jnp.float32
    )
    col_bits = lax.axis_size("col").bit_length() - 1
    row_bits = lax.axis_size("row").bit_length() - 1
    levels = col_bits + row_bits
    blocks = partial_value[INNER:].reshape(levels, SEP_COLS, width)
    blocks = col_rounds(blocks, levels)
    blocks = row_rounds(blocks, col_bits)
    coef = jnp.concatenate([partial_value[:INNER], blocks.reshape(-1, width)], axis=0).astype(
        jnp.bfloat16
    )
    return jnp.dot(x_factor, coef, preferred_element_type=jnp.float32)


def solution(mesh):
    placed = (
        P(("row", "col"), None, None),
        P(("row", "col"), None),
        P(("row", "col"), None, None),
        P(("row", "col"), None),
    )
    return jax.shard_map(
        per_device, mesh=mesh, in_specs=placed, out_specs=P(("row", "col"), None), check_vma=False
    )
```

profile of v0, /device:TPU:0, one launch (start us, length us, event | category | flops | bytes accessed | tf_op | source)
XLA Modules:
  0.0 46.4 jit_solution(419867413741520217)
XLA Ops:
  0.0 0.0 copy-start
  0.0 0.9 %copy.6 = s32[512,3]{1,0:T(8,128)S(1)} copy(s32[512,3]{0,1:T(4,128)} %param.5) | data formatting | bytes 12288 | tf_op args[1]
  0.9 0.2 eq.30
  1.1 1.8 %copy.7 = bf16[512,3,256]{2,1,0:T(4,128)(2,1)S(1)} copy(bf16[512,3,256]{2,0,1:T(8,128)(2,1)} %param.4) | data formatting | bytes 1572864 | tf_op args[0]
  3.0 0.0 copy-start.1
  3.0 0.7 %reshape.13 = bf16[1536,256]{1,0:T(8,128)(2,1)S(1)} reshape(bf16[512,3,256]{2,1,0:T(4,128)(2,1)S(1)} %copy.7) | data formatting | bytes 1572864 | tf_op jit(solution)/shard_map/reshape | solution.py:59
  3.7 0.5 %fusion = f32[384,256]{1,0:T(8,128)S(1)} fusion(bf16[1536,256]{1,0:T(8,128)(2,1)S(1)} %reshape.13, s32[1536]{0:T(1024)S(1)} %eq.30), kind=kOutput, calls=%fused_computation.2 | convolution fusion | flops 302579712 | bytes 1185792 | tf_op jit(solution)/shard_map/dot_general | solution.py:63
  4.2 3.0 %collective-permute-start = (f32[64,256]{1,0:T(8,128)S(1)}, f32[64,256]{1,0:T(8,128)S(1)}, u32[]{:S(2)}, u32[]{:S(2)}) collective-permute-start(f32[64,256]{1,0:T(8,128)S(1)} %get-tuple-element.11), channel_id=1, source_target_pairs={{0,1},{1,2},{2,3},{3,4},{4,5},{5,6},{6,7},{7,0},{8,9},{9,10},{10,1... | collective-permute-start | bytes 196616 | tf_op jit(solution)/shard_map/ppermute | solution.py:26
  7.2 3.1 %collective-permute-start.1 = (f32[64,256]{1,0:T(8,128)S(1)}, f32[64,256]{1,0:T(8,128)S(1)}, u32[]{:S(2)}, u32[]{:S(2)}) collective-permute-start(f32[64,256]{1,0:T(8,128)S(1)} %get-tuple-element.12), channel_id=1, source_target_pairs={{1,0},{2,1},{3,2},{4,3},{5,4},{6,5},{7,6},{0,7},{9,8},{10,9},{11,1... | collective-permute-start | bytes 196616 | tf_op jit(solution)/shard_map/ppermute | solution.py:29
  10.3 0.0 copy-done.1
  10.3 2.6 %collective-permute-done.1 = f32[64,256]{1,0:T(8,128)S(1)} collective-permute-done((f32[64,256]{1,0:T(8,128)S(1)}, f32[64,256]{1,0:T(8,128)S(1)}, u32[]{:S(2)}, u32[]{:S(2)}) %collective-permute-start.1) | collective-permute-done | bytes 65568 | tf_op jit(solution)/shard_map/ppermute | solution.py:29
  12.9 0.2 fusion.11
  13.1 0.0 collective-permute-done
  13.1 0.3 fusion.3
  13.4 0.0 copy-done
  13.4 0.4 convolution_bitcast_fusion
  13.8 1.1 %collective-permute-start.2 = (f32[5,64,256]{2,1,0:T(8,128)S(1)}, f32[5,64,256]{2,1,0:T(8,128)S(1)}, u32[]{:S(2)}, u32[]{:S(2)}) collective-permute-start(f32[5,64,256]{2,1,0:T(8,128)S(1)} %bitcast.16), channel_id=1, source_target_pairs={{0,1},{1,0},{2,3},{3,2},{4,5},{5,4},{6,7},{7,6},{8,9},{9,8},{10,11... | collective-permute-start | bytes 983048 | tf_op jit(solution)/shard_map/ppermute | solution.py:17
  15.0 7.0 %collective-permute-done.2 = f32[5,64,256]{2,1,0:T(8,128)S(1)} collective-permute-done((f32[5,64,256]{2,1,0:T(8,128)S(1)}, f32[5,64,256]{2,1,0:T(8,128)S(1)}, u32[]{:S(2)}, u32[]{:S(2)}) %collective-permute-start.2) | collective-permute-done | bytes 327712 | tf_op jit(solution)/shard_map/ppermute | solution.py:17
  22.0 1.9 %collective-permute-start.3 = (f32[4,64,256]{2,1,0:T(8,128)S(1)}, f32[4,64,256]{2,1,0:T(8,128)S(1)}, u32[]{:S(2)}, u32[]{:S(2)}) collective-permute-start(f32[4,64,256]{2,1,0:T(8,128)S(1)} %slice.78), channel_id=1, source_target_pairs={{0,2},{2,0},{1,3},{3,1},{4,6},{6,4},{5,7},{7,5},{8,10},{10,8},{9,1... | collective-permute-start | bytes 786440 | tf_op jit(solution)/shard_map/ppermute | solution.py:17
  23.9 5.2 %collective-permute-done.3 = f32[4,64,256]{2,1,0:T(8,128)S(1)} collective-permute-done((f32[4,64,256]{2,1,0:T(8,128)S(1)}, f32[4,64,256]{2,1,0:T(8,128)S(1)}, u32[]{:S(2)}, u32[]{:S(2)}) %collective-permute-start.3) | collective-permute-done | bytes 262176 | tf_op jit(solution)/shard_map/ppermute | solution.py:17
  29.2 2.8 %collective-permute-start.4 = (f32[3,64,256]{2,1,0:T(8,128)S(1)}, f32[3,64,256]{2,1,0:T(8,128)S(1)}, u32[]{:S(2)}, u32[]{:S(2)}) collective-permute-start(f32[3,64,256]{2,1,0:T(8,128)S(1)} %slice.79), channel_id=1, source_target_pairs={{0,4},{4,0},{1,5},{5,1},{2,6},{6,2},{3,7},{7,3},{8,12},{12,8},{9,1... | collective-permute-start | bytes 589832 | tf_op jit(solution)/shard_map/ppermute | solution.py:17
  32.1 7.2 %collective-permute-done.4 = f32[3,64,256]{2,1,0:T(8,128)S(1)} collective-permute-done((f32[3,64,256]{2,1,0:T(8,128)S(1)}, f32[3,64,256]{2,1,0:T(8,128)S(1)}, u32[]{:S(2)}, u32[]{:S(2)}) %collective-permute-start.4) | collective-permute-done | bytes 196640 | tf_op jit(solution)/shard_map/ppermute | solution.py:17
  39.3 0.1 collective-permute-start.5
  39.4 0.1 slice.91
  39.5 1.2 %collective-permute-done.5 = f32[2,64,256]{2,1,0:T(8,128)S(1)} collective-permute-done((f32[2,64,256]{2,1,0:T(8,128)S(1)}, f32[2,64,256]{2,1,0:T(8,128)S(1)}, u32[]{:S(2)}, u32[]{:S(2)}) %collective-permute-start.5) | collective-permute-done | bytes 131104 | tf_op jit(solution)/shard_map/ppermute | solution.py:17
  40.8 1.5 %collective-permute-start.6 = (f32[1,64,256]{2,1,0:T(8,128)S(1)}, f32[1,64,256]{2,1,0:T(8,128)S(1)}, u32[]{:S(2)}, u32[]{:S(2)}) collective-permute-start(f32[1,64,256]{2,1,0:T(8,128)S(1)} %slice.81), channel_id=1, source_target_pairs={{0,16},{16,0},{8,24},{24,8},{1,17},{17,1},{9,25},{25,9},{2,18},{18... | collective-permute-start | bytes 196616 | tf_op jit(solution)/shard_map/ppermute | solution.py:17
  42.3 2.8 %collective-permute-done.6 = f32[1,64,256]{2,1,0:T(8,128)S(1)} collective-permute-done((f32[1,64,256]{2,1,0:T(8,128)S(1)}, f32[1,64,256]{2,1,0:T(8,128)S(1)}, u32[]{:S(2)}, u32[]{:S(2)}) %collective-permute-start.6) | collective-permute-done | bytes 65568 | tf_op jit(solution)/shard_map/ppermute | solution.py:17
  45.1 0.4 convolution_bitcast_fusion.1
  45.6 0.8 %copy.8 = f32[256,256]{1,0:T(8,128)} copy(f32[256,256]{0,1:T(8,128)S(1)} %convolution_bitcast_fusion.1) | data formatting | bytes 524288 | tf_op jit(solution)/shard_map/dot_general | solution.py:90
  (15 shorter events, 0.3 us)
Async XLA Ops:
  0.0 13.4 %copy-start = (bf16[256,1728]{0,1:T(8,128)(2,1)S(1)}, bf16[256,1728]{0,1:T(8,128)(2,1)}, u32[]{:S(2)}) copy-start(bf16[256,1728]{0,1:T(8,128)(2,1)} %param.7) | copy-start | bytes 2654212
  3.0 7.4 %copy-start.1 = (s32[1,2,64]{2,1,0:T(2,128)S(1)}, s32[1,2,64]{2,1,0:T(2,128)}, u32[]{:S(2)}) copy-start(s32[1,2,64]{2,1,0:T(2,128)} %param.6) | copy-start | bytes 1540
  4.2 9.0 %collective-permute-start = (f32[64,256]{1,0:T(8,128)S(1)}, f32[64,256]{1,0:T(8,128)S(1)}, u32[]{:S(2)}, u32[]{:S(2)}) collective-permute-start(f32[64,256]{1,0:T(8,128)S(1)} %get-tuple-element.11), channel_id=1, source_target_pairs={{0,1},{1,2},{2,3},{3,4},{4,5},{5,6},{6,7},{7,0},{8,9},{9,10},{10,1... | collective-permute-start | bytes 196616 | tf_op jit(solution)/shard_map/ppermute | solution.py:26
  7.2 5.7 %collective-permute-start.1 = (f32[64,256]{1,0:T(8,128)S(1)}, f32[64,256]{1,0:T(8,128)S(1)}, u32[]{:S(2)}, u32[]{:S(2)}) collective-permute-start(f32[64,256]{1,0:T(8,128)S(1)} %get-tuple-element.12), channel_id=1, source_target_pairs={{1,0},{2,1},{3,2},{4,3},{5,4},{6,5},{7,6},{0,7},{9,8},{10,9},{11,1... | collective-permute-start | bytes 196616 | tf_op jit(solution)/shard_map/ppermute | solution.py:29
  13.8 8.1 %collective-permute-start.2 = (f32[5,64,256]{2,1,0:T(8,128)S(1)}, f32[5,64,256]{2,1,0:T(8,128)S(1)}, u32[]{:S(2)}, u32[]{:S(2)}) collective-permute-start(f32[5,64,256]{2,1,0:T(8,128)S(1)} %bitcast.16), channel_id=1, source_target_pairs={{0,1},{1,0},{2,3},{3,2},{4,5},{5,4},{6,7},{7,6},{8,9},{9,8},{10,11... | collective-permute-start | bytes 983048 | tf_op jit(solution)/shard_map/ppermute | solution.py:17
  22.0 7.1 %collective-permute-start.3 = (f32[4,64,256]{2,1,0:T(8,128)S(1)}, f32[4,64,256]{2,1,0:T(8,128)S(1)}, u32[]{:S(2)}, u32[]{:S(2)}) collective-permute-start(f32[4,64,256]{2,1,0:T(8,128)S(1)} %slice.78), channel_id=1, source_target_pairs={{0,2},{2,0},{1,3},{3,1},{4,6},{6,4},{5,7},{7,5},{8,10},{10,8},{9,1... | collective-permute-start | bytes 786440 | tf_op jit(solution)/shard_map/ppermute | solution.py:17
  29.2 10.1 %collective-permute-start.4 = (f32[3,64,256]{2,1,0:T(8,128)S(1)}, f32[3,64,256]{2,1,0:T(8,128)S(1)}, u32[]{:S(2)}, u32[]{:S(2)}) collective-permute-start(f32[3,64,256]{2,1,0:T(8,128)S(1)} %slice.79), channel_id=1, source_target_pairs={{0,4},{4,0},{1,5},{5,1},{2,6},{6,2},{3,7},{7,3},{8,12},{12,8},{9,1... | collective-permute-start | bytes 589832 | tf_op jit(solution)/shard_map/ppermute | solution.py:17
  39.3 1.4 %collective-permute-start.5 = (f32[2,64,256]{2,1,0:T(8,128)S(1)}, f32[2,64,256]{2,1,0:T(8,128)S(1)}, u32[]{:S(2)}, u32[]{:S(2)}) collective-permute-start(f32[2,64,256]{2,1,0:T(8,128)S(1)} %slice.80), channel_id=1, source_target_pairs={{0,8},{8,0},{16,24},{24,16},{1,9},{9,1},{17,25},{25,17},{2,10},{10... | collective-permute-start | bytes 393224 | tf_op jit(solution)/shard_map/ppermute | solution.py:17
  40.8 4.3 %collective-permute-start.6 = (f32[1,64,256]{2,1,0:T(8,128)S(1)}, f32[1,64,256]{2,1,0:T(8,128)S(1)}, u32[]{:S(2)}, u32[]{:S(2)}) collective-permute-start(f32[1,64,256]{2,1,0:T(8,128)S(1)} %slice.81), channel_id=1, source_target_pairs={{0,16},{16,0},{8,24},{24,8},{1,17},{17,1},{9,25},{25,9},{2,18},{18... | collective-permute-start | bytes 196616 | tf_op jit(solution)/shard_map/ppermute | solution.py:17
where the time goes:
time: 46.6 us; the launch traced here: 46.4 us
  waiting for transfers between devices  26 us (56%)
  starting transfers between devices  13.6 us (29%)
  local copies, waits for them, and re-layouts  4.65 us (10%)
  matrix products  1.83 us (4%)
    ppermute x5, waiting for transfers between devices, swapped(): return lax.ppermute(block, axis, route)  23.5 us
    ppermute x5, starting transfers between devices, swapped(): return lax.ppermute(block, axis, route)  7.46 us
    ppermute x1, starting transfers between devices, padded_2(): lax.ppermute(lax.slice_in_dim(block, 0, width, axis=dim), axis, backward)  3.1 us
    ppermute x1, starting transfers between devices, padded_2(): lax.ppermute(lax.slice_in_dim(block, block.shape[dim] - width, None, axis...  3.03 us
    unnamed x6, local copies, waits for them, and re-layouts  2.74 us
    ppermute x1, waiting for transfers between devices, padded_2(): lax.ppermute(lax.slice_in_dim(block, 0, width, axis=dim), axis, backward)  2.57 us
  transfers between devices with their start and end apart: 7, of which 6 were waited for; matrix products, arithmetic and copies ran while one was open for 1% of the time, Pallas kernels for 0%

commit v1 on v0

v1 whole, which is shorter than its diff:
```python
import functools

import jax
import jax.numpy as jnp
from jax import lax
from jax.experimental import pallas as pl
from jax.experimental.pallas import tpu as pltpu
from jax.sharding import PartitionSpec as P

INNER = 1408
MESH = pl.DeviceIdType.MESH
F32 = jnp.float32
BF16 = jnp.bfloat16


def swapped(block, axis, stride):
    count = lax.axis_size(axis)
    route = []
    for low in range(count):
        high = low | 1 << stride
        if high != low and high < count:
            route += [(low, high), (high, low)]
    return lax.ppermute(block, axis, route)


def summed_levels(blocks, n_row, n_col):
    col_bits = n_col.bit_length() - 1
    row_bits = n_row.bit_length() - 1
    for bit in range(col_bits + row_bits):
        axis, stride = ("col", bit) if bit < col_bits else ("row", bit - col_bits)
        partner = swapped(blocks[bit:], axis, stride)
        blocks = jnp.concatenate([blocks[:bit], blocks[bit:] + partner], axis=0)
    return blocks


def by_rounds(n_row, n_col, elem_residual, corners, share_rows, x_factor):
    rows_dev = x_factor.shape[0]
    shared = share_rows.shape[2]
    width = elem_residual.shape[2]
    levels = (n_row * n_col).bit_length() - 1
    ext_len = rows_dev + 2 * shared
    flat_ids = corners.reshape(-1)
    onehot = (
        lax.broadcasted_iota(jnp.int32, (ext_len, flat_ids.shape[0]), 0) == flat_ids[None, :]
    ).astype(BF16)
    extended = jnp.dot(onehot, elem_residual.reshape(-1, width), preferred_element_type=F32)
    forward = [(i, (i + 1) % n_col) for i in range(n_col)]
    backward = [(target, source) for source, target in forward]
    from_left = lax.ppermute(extended[rows_dev + shared :], "col", forward)
    from_right = lax.ppermute(extended[rows_dev : rows_dev + shared], "col", backward)
    row_ids = lax.broadcasted_iota(jnp.int32, (rows_dev, shared), 0)
    assembled = extended[:rows_dev]
    for side, received in ((0, from_left), (1, from_right)):
        side_map = (row_ids == share_rows[0, side][None, :]).astype(F32)
        assembled = assembled + jnp.dot(
            side_map, received, precision=lax.Precision.HIGHEST, preferred_element_type=F32
        )
    partial_value = lax.dot_general(
        x_factor, assembled.astype(BF16), (((0,), (0,)), ((), ())), preferred_element_type=F32
    )
    blocks = partial_value[INNER:].reshape(levels, -1, width)
    blocks = summed_levels(blocks, n_row, n_col)
    coef = jnp.concatenate([partial_value[:INNER], blocks.reshape(-1, width)], axis=0)
    return jnp.dot(x_factor, coef.astype(BF16), preferred_element_type=F32)


class Plan:
    def __init__(self, n_row, n_col, sep):
        self.n_row, self.n_col, self.sep = n_row, n_col, sep
        self.n_z = n_col // 2
        self.levels = (n_row * n_col).bit_length() - 1

    def z_span(self, level):
        return min(2 ** (level - 1), self.n_z)

    def row_span(self, level):
        return max(1, 2**level // self.n_col)

    def piece(self, level):
        return self.sep // self.z_span(level)


def takes(n_row, n_col, sep):
    return n_col >= 4 and n_row <= 4 and sep % (8 * (n_col // 2)) == 0


def tdot(a, b):
    return lax.dot_general(a, b, (((0,), (0,)), ((), ())), preferred_element_type=F32)


def kernel(
    plan,
    er_hbm, cor_hbm, sh_hbm, x_hbm,
    out_ref,
    er, cor, sh, xt,
    halo_out, halo_in, own, rhs, part, l1_in, rs_in, ex_out, ex_in, final,
    in_sem, halo_s, halo_r, l1_s, l1_r, rs_s, rs_r, ex_s, ex_r, ag_s, ag_r,
):
    row, col = lax.axis_index("row"), lax.axis_index("col")
    z, x = col // 2, col % 2
    levels, n_col = plan.levels, plan.n_col
    rows_dev = out_ref.shape[0]
    shared = halo_out.shape[1]
    kinds = er.shape[0]
    elems = er.shape[1]
    inner = xt.shape[0] - plan.sep * levels

    loads = [
        pltpu.make_async_copy(source, target, in_sem.at[i])
        for i, (source, target) in enumerate(
            ((cor_hbm, cor), (er_hbm, er), (sh_hbm, sh), (x_hbm, xt))
        )
    ]
    for load in loads:
        load.start()

    right = (row, (col + 1) % n_col)
    left = (row, (col + n_col - 1) % n_col)

    def z_peer(level, m):
        span = plan.z_span(level)
        local = z % span
        return (row, (z - local + (local + m) % span) * 2 + x)

    def side_peer(level, a, k):
        span = plan.row_span(level)
        local = row % span
        return (row - local + (local + k) % span, z * 2 + (x + a) % 2)

    top = levels
    greeted = [left, right]
    greeted += [z_peer(top, m) for m in range(1, plan.n_z)]
    greeted += [
        side_peer(top, a, k)
        for a in range(2)
        for k in range(plan.row_span(top))
        if a or k
    ]
    barrier = pltpu.get_barrier_semaphore()
    for peer in greeted:
        pl.semaphore_signal(barrier, inc=1, device_id=peer, device_id_type=MESH)

    def assembled_rows(start, count):
        total = None
        for k in range(kinds):
            ids = cor[k : k + 1, :]
            at = lax.broadcasted_iota(jnp.int32, (count, elems), 0) + start
            onehot = jnp.where(at == ids, 1.0, 0.0).astype(BF16)
            term = jnp.dot(onehot, er[k], preferred_element_type=F32)
            total = term if total is None else total + term
        return total

    loads[0].wait()
    loads[1].wait()
    halo_out[...] = assembled_rows(rows_dev, 2 * shared).reshape(halo_out.shape)
    pl.semaphore_wait(barrier, len(greeted))

    def remote(source, target, send, recv, peer):
        copy = pltpu.make_async_remote_copy(
            src_ref=source,
            dst_ref=target,
            send_sem=send,
            recv_sem=recv,
            device_id=peer,
            device_id_type=MESH,
        )
        copy.start()
        return copy

    sent = []
    halo = [
        remote(halo_out.at[1], halo_in.at[0], halo_s.at[0], halo_r.at[0], right),
        remote(halo_out.at[0], halo_in.at[1], halo_s.at[1], halo_r.at[1], left),
    ]
    sent += halo

    own[...] = assembled_rows(0, rows_dev)
    loads[2].wait()
    targets = jnp.concatenate([sh[0:1, :], sh[1:2, :]], axis=1)
    at = lax.broadcasted_iota(jnp.int32, (rows_dev, 2 * shared), 0)
    share_map = jnp.where(at == targets, 1.0, 0.0).astype(BF16)
    share_map = jnp.concatenate([share_map, share_map], axis=1)
    loads[3].wait()
    for copy in halo:
        copy.wait_recv()
    received = halo_in[...].reshape(2 * shared, -1)
    high = received.astype(BF16)
    low = (received - high.astype(F32)).astype(BF16)
    received = jnp.concatenate([high, low], axis=0)
    assembled = own[...] + jnp.dot(share_map, received, preferred_element_type=F32)
    rhs[...] = assembled.astype(BF16)
    part[...] = jnp.dot(xt[inner:, :], rhs[...], preferred_element_type=F32).reshape(part.shape)

    rs, ex, ag = {}, {}, {}
    order = list(range(levels, 1, -1))
    for level in order:
        span, rows = plan.z_span(level), plan.piece(level)
        for m in range(1, span):
            index = (z % span + m) % span
            rs[level, m] = remote(
                part.at[level - 1, pl.ds(pl.multiple_of(index * rows, 8), rows)],
                rs_in.at[level - 1, m - 1, pl.ds(0, rows)],
                rs_s.at[level - 1, m - 1],
                rs_r.at[level - 1, m - 1],
                z_peer(level, m),
            )
    first = remote(part.at[0], l1_in, l1_s.at[0], l1_r.at[0], side_peer(1, 1, 0))
    sent += list(rs.values()) + [first]

    weights = jnp.dot(xt[:inner, :], rhs[...], preferred_element_type=F32).astype(BF16)
    out_ref[...] = tdot(xt[:inner, :], weights)

    for level in order:
        span, rows = plan.z_span(level), plan.piece(level)
        mine = pl.ds(pl.multiple_of((z % span) * rows, 8), rows)
        total = part[level - 1, mine]
        for m in range(1, span):
            rs[level, m].wait_recv()
            total = total + rs_in[level - 1, m - 1, pl.ds(0, rows)]
        ex_out[level - 1, pl.ds(0, rows)] = total
        r_span = plan.row_span(level)
        for a in range(2):
            for k in range(r_span):
                if a or k:
                    slot = a * r_span + k - 1
                    ex[level, a, k] = remote(
                        ex_out.at[level - 1, pl.ds(0, rows)],
                        ex_in.at[level - 1, slot, pl.ds(0, rows)],
                        ex_s.at[level - 1, slot],
                        ex_r.at[level - 1, slot],
                        side_peer(level, a, k),
                    )
    sent += list(ex.values())
    for level in order:
        span, rows = plan.z_span(level), plan.piece(level)
        mine = pl.ds(pl.multiple_of((z % span) * rows, 8), rows)
        total = ex_out[level - 1, pl.ds(0, rows)]
        r_span = plan.row_span(level)
        for a in range(2):
            for k in range(r_span):
                if a or k:
                    ex[level, a, k].wait_recv()
                    total = total + ex_in[level - 1, a * r_span + k - 1, pl.ds(0, rows)]
        final[level - 1, mine] = total
        for m in range(1, span):
            ag[level, m] = remote(
                final.at[level - 1, mine],
                final.at[level - 1, mine],
                ag_s.at[level - 1, m - 1],
                ag_r.at[level - 1, m - 1],
                z_peer(level, m),
            )
    sent += list(ag.values())
    first.wait_recv()
    final[0] = part[0] + l1_in[...]
    for copy in ag.values():
        copy.wait_recv()
    coef = final[...].reshape(plan.sep * levels, -1).astype(BF16)
    out_ref[...] += tdot(xt[inner:, :], coef)
    for copy in sent:
        copy.wait_send()


def in_one_kernel(plan, elem_residual, corners, share_rows, x_factor):
    rows_dev, cols = x_factor.shape
    shared = share_rows.shape[2]
    elems, kinds, width = elem_residual.shape
    levels, sep = plan.levels, plan.sep
    top = plan.row_span(levels) * 2 - 1
    z_slots = plan.n_z - 1
    half = sep // 2
    dma = pltpu.SemaphoreType.DMA
    anywhere = pl.BlockSpec(memory_space=pl.ANY)
    return pl.pallas_call(
        functools.partial(kernel, plan),
        out_shape=jax.ShapeDtypeStruct((rows_dev, width), F32),
        in_specs=[anywhere] * 4,
        out_specs=pl.BlockSpec(memory_space=pltpu.VMEM),
        scratch_shapes=[
            pltpu.VMEM((kinds, elems, width), BF16),
            pltpu.VMEM((kinds, elems), jnp.int32),
            pltpu.VMEM((2, shared), jnp.int32),
            pltpu.VMEM((cols, rows_dev), BF16),
            pltpu.VMEM((2, shared, width), F32),
            pltpu.VMEM((2, shared, width), F32),
            pltpu.VMEM((rows_dev, width), F32),
            pltpu.VMEM((rows_dev, width), BF16),
            pltpu.VMEM((levels, sep, width), F32),
            pltpu.VMEM((sep, width), F32),
            pltpu.VMEM((levels, z_slots, half, width), F32),
            pltpu.VMEM((levels, half, width), F32),
            pltpu.VMEM((levels, top, half, width), F32),
            pltpu.VMEM((levels, sep, width), F32),
            dma((4,)),
            dma((2,)),
            dma((2,)),
            dma((1,)),
            dma((1,)),
            dma((levels, z_slots)),
            dma((levels, z_slots)),
            dma((levels, top)),
            dma((levels, top)),
            dma((levels, z_slots)),
            dma((levels, z_slots)),
        ],
        compiler_params=pltpu.CompilerParams(collective_id=0, has_side_effects=True),
        name="factor_solve",
    )(
        elem_residual.transpose(1, 0, 2),
        corners.T,
        share_rows.reshape(2, shared),
        x_factor.T,
    )


def solution(mesh):
    n_row, n_col = mesh.shape["row"], mesh.shape["col"]
    levels = (n_row * n_col).bit_length() - 1

    def per_device(elem_residual, corners, share_rows, x_factor):
        sep = (x_factor.shape[1] - INNER) // levels
        args = (elem_residual, corners, share_rows, x_factor)
        if takes(n_row, n_col, sep):
            return in_one_kernel(Plan(n_row, n_col, sep), *args)
        return by_rounds(n_row, n_col, *args)

    placed = (
        P(("row", "col"), None, None),
        P(("row", "col"), None),
        P(("row", "col"), None, None),
        P(("row", "col"), None),
    )
    return jax.shard_map(
        per_device, mesh=mesh, in_specs=placed, out_specs=P(("row", "col"), None), check_vma=False
    )
```

time: 46.6 us -> 28.7 us (0.62)
  Pallas kernels: 0 us -> 26.8 us
  waiting for transfers between devices: 26 us -> 0 us
  starting transfers between devices: 13.6 us -> 0 us
  local copies, waits for them, and re-layouts: 4.65 us -> 1.67 us
  matrix products: 1.83 us -> 0 us
    pallas_call x0 -> x1, Pallas kernels: none -> 26.8 us  [in_one_kernel(): pl.pallas_call(functools.partial(kernel, plan), out_shape=jax.ShapeDtypeS...]
    ppermute x7 -> x0, waiting for transfers between devices: 26 us -> none  [the longest x5 23.5 us: swapped(): return lax.ppermute(block, axis, route)]
    ppermute x7 -> x0, starting transfers between devices: 13.6 us -> none  [the longest x5 7.46 us: swapped(): return lax.ppermute(block, axis, route)]
    dot_general x5 -> x0, matrix products: 1.83 us -> none  [the longest x1 0.48 us: per_device(): extended = jnp.dot(onehot, values, preferred_element_type=jnp.float32)]
    unnamed x6 -> x1, local copies, waits for them, and re-layouts: 2.74 us -> 1.67 us
    dot_general x1 -> x0, local copies, waits for them, and re-layouts: 0.84 us -> none  [per_device(): return jnp.dot(x_factor, coef, preferred_element_type=jnp.float32)]
    reshape x1 -> x0, local copies, waits for them, and re-layouts: 0.7 us -> none  [per_device(): values = elem_residual.reshape(-1, width)]
  transfers between devices with their start and end apart: 7 -> 0, of which waited for: 6 -> 0; matrix products, arithmetic and copies ran while one was open for 1% -> 0% of each run, Pallas kernels for 0% -> 0%
where the time goes in v1:
time: 28.7 us; the launch traced here: 28.5 us
  Pallas kernels  26.8 us (93%)
  local copies, waits for them, and re-layouts  1.67 us (6%)
    pallas_call x1, Pallas kernels, in_one_kernel(): pl.pallas_call(functools.partial(kernel, plan), out_shape=jax.ShapeDtypeS...  26.8 us
    unnamed x1, local copies, waits for them, and re-layouts  1.67 us

profile of v1, /device:TPU:0, one launch (start us, length us, event | category | flops | bytes accessed | tf_op | source)
XLA Modules:
  0.0 28.5 jit_solution(8715665289999136946)
XLA Ops:
  0.0 26.8 %factor_solve.1 = f32[256,256]{1,0:T(8,128)} custom-call(bf16[3,512,256]{2,1,0:T(8,128)(2,1)} %bitcast.5, s32[3,512]{1,0:T(4,128)} %bitcast.6, s32[2,64]{1,0:T(2,128)} %bitcast.7, bf16[1728,256]{1,0:T(8,128)(2,1)} %bitcast.4), custom_call_target="tpu_custom_call" | custom-call | tf_op jit(solution)/shard_map/factor_solve/pallas_call | solution.py:274
  26.8 1.7 %copy.6 = f32[256,256]{1,0:T(8,128)} copy(f32[256,256]{1,0:T(8,128)} %factor_solve.1) | data formatting | bytes 524288

commit v2 on v1

--- a/solution.py
+++ b/solution.py
@@ -67,21 +67,25 @@
 class Plan:
     def __init__(self, n_row, n_col, sep):
         self.n_row, self.n_col, self.sep = n_row, n_col, sep
-        self.n_z = n_col // 2
         self.levels = (n_row * n_col).bit_length() - 1
-
-    def z_span(self, level):
-        return min(2 ** (level - 1), self.n_z)
+        self.col_bits = n_col.bit_length() - 1
+        self.groups = []
+        if self.levels > self.col_bits:
+            self.groups.append((self.col_bits + 1, self.levels))
+        self.groups += [(level, level) for level in range(self.col_bits, 1, -1)]
+
+    def span(self, level):
+        return min(2**level, self.n_col)
 
     def row_span(self, level):
         return max(1, 2**level // self.n_col)
 
     def piece(self, level):
-        return self.sep // self.z_span(level)
+        return self.sep // self.span(level)
 
 
 def takes(n_row, n_col, sep):
-    return n_col >= 4 and n_row <= 4 and sep % (8 * (n_col // 2)) == 0
+    return n_col >= 4 and 2 <= n_row <= 4 and sep % (8 * n_col) == 0
 
 
 def tdot(a, b):
@@ -97,13 +101,29 @@
     in_sem, halo_s, halo_r, l1_s, l1_r, rs_s, rs_r, ex_s, ex_r, ag_s, ag_r,
 ):
     row, col = lax.axis_index("row"), lax.axis_index("col")
-    z, x = col // 2, col % 2
     levels, n_col = plan.levels, plan.n_col
     rows_dev = out_ref.shape[0]
     shared = halo_out.shape[1]
     kinds = er.shape[0]
     elems = er.shape[1]
     inner = xt.shape[0] - plan.sep * levels
+
+    right = (row, (col + 1) % n_col)
+    left = (row, (col + n_col - 1) % n_col)
+
+    def col_peer(span, m):
+        local = col % span
+        return (row, col - local + (local + m) % span)
+
+    def row_peer(span, k):
+        local = row % span
+        return (row - local + (local + k) % span, col)
+
+    greeted = [col_peer(n_col, m) for m in range(1, n_col)]
+    greeted += [row_peer(plan.n_row, k) for k in range(1, plan.n_row)]
+    barrier = pltpu.get_barrier_semaphore()
+    for peer in greeted:
+        pl.semaphore_signal(barrier, inc=1, device_id=peer, device_id_type=MESH)
 
     loads = [
         pltpu.make_async_copy(source, target, in_sem.at[i])
@@ -113,32 +133,6 @@
     ]
     for load in loads:
         load.start()
-
-    right = (row, (col + 1) % n_col)
-    left = (row, (col + n_col - 1) % n_col)
-
-    def z_peer(level, m):
-        span = plan.z_span(level)
-        local = z % span
-        return (row, (z - local + (local + m) % span) * 2 + x)
-
-    def side_peer(level, a, k):
-        span = plan.row_span(level)
-        local = row % span
-        return (row - local + (local + k) % span, z * 2 + (x + a) % 2)
-
-    top = levels
-    greeted = [left, right]
-    greeted += [z_peer(top, m) for m in range(1, plan.n_z)]
-    greeted += [
-        side_peer(top, a, k)
-        for a in range(2)
-        for k in range(plan.row_span(top))
-        if a or k
-    ]
-    barrier = pltpu.get_barrier_semaphore()
-    for peer in greeted:
-        pl.semaphore_signal(barrier, inc=1, device_id=peer, device_id_type=MESH)
 
     def assembled_rows(start, count):
         total = None
@@ -153,6 +147,7 @@
     loads[0].wait()
     loads[1].wait()
     halo_out[...] = assembled_rows(rows_dev, 2 * shared).reshape(halo_out.shape)
+    own[...] = assembled_rows(0, rows_dev)
     pl.semaphore_wait(barrier, len(greeted))
 
     def remote(source, target, send, recv, peer):
@@ -174,7 +169,6 @@
     ]
     sent += halo
 
-    own[...] = assembled_rows(0, rows_dev)
     loads[2].wait()
     targets = jnp.concatenate([sh[0:1, :], sh[1:2, :]], axis=1)
     at = lax.broadcasted_iota(jnp.int32, (rows_dev, 2 * shared), 0)
@@ -191,65 +185,76 @@
     rhs[...] = assembled.astype(BF16)
     part[...] = jnp.dot(xt[inner:, :], rhs[...], preferred_element_type=F32).reshape(part.shape)
 
+    def own_rows(level, ahead=0):
+        span, rows = plan.span(level), plan.piece(level)
+        return pl.ds(pl.multiple_of((col % span + ahead) % span * rows, 8), rows)
+
     rs, ex, ag = {}, {}, {}
-    order = list(range(levels, 1, -1))
-    for level in order:
-        span, rows = plan.z_span(level), plan.piece(level)
-        for m in range(1, span):
-            index = (z % span + m) % span
-            rs[level, m] = remote(
-                part.at[level - 1, pl.ds(pl.multiple_of(index * rows, 8), rows)],
-                rs_in.at[level - 1, m - 1, pl.ds(0, rows)],
-                rs_s.at[level - 1, m - 1],
-                rs_r.at[level - 1, m - 1],
-                z_peer(level, m),
+    for low, high in plan.groups:
+        count = high - low + 1
+        for m in range(1, plan.span(low)):
+            rs[low, m] = remote(
+                part.at[pl.ds(low - 1, count), own_rows(low, m)],
+                rs_in.at[m - 1, pl.ds(low - 1, count), pl.ds(0, plan.piece(low))],
+                rs_s.at[low - 1, m - 1],
+                rs_r.at[low - 1, m - 1],
+                col_peer(plan.span(low), m),
             )
-    first = remote(part.at[0], l1_in, l1_s.at[0], l1_r.at[0], side_peer(1, 1, 0))
+    first = remote(part.at[0], l1_in, l1_s.at[0], l1_r.at[0], col_peer(2, 1))
     sent += list(rs.values()) + [first]
 
     weights = jnp.dot(xt[:inner, :], rhs[...], preferred_element_type=F32).astype(BF16)
     out_ref[...] = tdot(xt[:inner, :], weights)
 
-    for level in order:
-        span, rows = plan.z_span(level), plan.piece(level)
-        mine = pl.ds(pl.multiple_of((z % span) * rows, 8), rows)
-        total = part[level - 1, mine]
-        for m in range(1, span):
-            rs[level, m].wait_recv()
-            total = total + rs_in[level - 1, m - 1, pl.ds(0, rows)]
-        ex_out[level - 1, pl.ds(0, rows)] = total
-        r_span = plan.row_span(level)
-        for a in range(2):
-            for k in range(r_span):
-                if a or k:
-                    slot = a * r_span + k - 1
-                    ex[level, a, k] = remote(
-                        ex_out.at[level - 1, pl.ds(0, rows)],
-                        ex_in.at[level - 1, slot, pl.ds(0, rows)],
-                        ex_s.at[level - 1, slot],
-                        ex_r.at[level - 1, slot],
-                        side_peer(level, a, k),
+    def gather(low, high):
+        count = high - low + 1
+        block = final.at[pl.ds(low - 1, count), own_rows(low)]
+        for m in range(1, plan.span(low)):
+            ag[low, m] = remote(
+                block,
+                block,
+                ag_s.at[low - 1, m - 1],
+                ag_r.at[low - 1, m - 1],
+                col_peer(plan.span(low), m),
+            )
+
+    for low, high in plan.groups:
+        rows = plan.piece(low)
+        for m in range(1, plan.span(low)):
+            rs[low, m].wait_recv()
+        for level in range(low, high + 1):
+            total = part[level - 1, own_rows(level)]
+            for m in range(1, plan.span(low)):
+                total = total + rs_in[m - 1, level - 1, pl.ds(0, rows)]
+            if level <= plan.col_bits:
+                final[level - 1, own_rows(level)] = total
+            else:
+                ex_out[level - plan.col_bits - 1] = total
+        if low <= plan.col_bits:
+            gather(low, high)
+            continue
+        for k in range(1, plan.n_row):
+            for level in range(low, high + 1):
+                if k < plan.row_span(level):
+                    at_level = level - plan.col_bits - 1
+                    ex[level, k] = remote(
+                        ex_out.at[at_level],
+                        ex_in.at[at_level, k - 1],
+                        ex_s.at[at_level, k - 1],
+                        ex_r.at[at_level, k - 1],
+                        row_peer(plan.row_span(level), k),
                     )
     sent += list(ex.values())
-    for level in order:
-        span, rows = plan.z_span(level), plan.piece(level)
-        mine = pl.ds(pl.multiple_of((z % span) * rows, 8), rows)
-        total = ex_out[level - 1, pl.ds(0, rows)]
-        r_span = plan.row_span(level)
-        for a in range(2):
-            for k in range(r_span):
-                if a or k:
-                    ex[level, a, k].wait_recv()
-                    total = total + ex_in[level - 1, a * r_span + k - 1, pl.ds(0, rows)]
-        final[level - 1, mine] = total
-        for m in range(1, span):
-            ag[level, m] = remote(
-                final.at[level - 1, mine],
-                final.at[level - 1, mine],
-                ag_s.at[level - 1, m - 1],
-                ag_r.at[level - 1, m - 1],
-                z_peer(level, m),
-            )
+    if plan.levels > plan.col_bits:
+        low, high = plan.groups[0]
+        for level in range(low, high + 1):
+            at_level = level - plan.col_bits - 1
+            total = ex_out[at_level]
+            for k in range(1, plan.row_span(level)):
+                ex[level, k].wait_recv()
+                total = total + ex_in[at_level, k - 1]
+            final[level - 1, own_rows(level)] = total
+        gather(low, high)
     sent += list(ag.values())
     first.wait_recv()
     final[0] = part[0] + l1_in[...]
@@ -266,9 +271,11 @@
     shared = share_rows.shape[2]
     elems, kinds, width = elem_residual.shape
     levels, sep = plan.levels, plan.sep
-    top = plan.row_span(levels) * 2 - 1
-    z_slots = plan.n_z - 1
-    half = sep // 2
+    slots = plan.n_col - 1
+    row_levels = levels - plan.col_bits
+    row_slots = plan.n_row - 1
+    half = sep // 4
+    small = sep // plan.n_col
     dma = pltpu.SemaphoreType.DMA
     anywhere = pl.BlockSpec(memory_space=pl.ANY)
     return pl.pallas_call(
@@ -287,21 +294,21 @@
             pltpu.VMEM((rows_dev, width), BF16),
             pltpu.VMEM((levels, sep, width), F32),
             pltpu.VMEM((sep, width), F32),
-            pltpu.VMEM((levels, z_slots, half, width), F32),
-            pltpu.VMEM((levels, half, width), F32),
-            pltpu.VMEM((levels, top, half, width), F32),
+            pltpu.VMEM((slots, levels, half, width), F32),
+            pltpu.VMEM((row_levels, small, width), F32),
+            pltpu.VMEM((row_levels, row_slots, small, width), F32),
             pltpu.VMEM((levels, sep, width), F32),
             dma((4,)),
             dma((2,)),
             dma((2,)),
             dma((1,)),
             dma((1,)),
-            dma((levels, z_slots)),
-            dma((levels, z_slots)),
-            dma((levels, top)),
-            dma((levels, top)),
-            dma((levels, z_slots)),
-            dma((levels, z_slots)),
+            dma((levels, slots)),
+            dma((levels, slots)),
+            dma((row_levels, row_slots)),
+            dma((row_levels, row_slots)),
+            dma((levels, slots)),
+            dma((levels, slots)),
         ],
         compiler_params=pltpu.CompilerParams(collective_id=0, has_side_effects=True),
         name="factor_solve",

time: 28.7 us -> 27.9 us (0.972)
  Pallas kernels: 26.8 us -> 26 us
    pallas_call x1, Pallas kernels: 26.8 us -> 26 us  [in_one_kernel(): pl.pallas_call(functools.partial(kernel, plan), out_shape=jax.ShapeDtypeS...]
where the time goes in v2:
time: 27.9 us; the launch traced here: 27.7 us
  Pallas kernels  26 us (93%)
  local copies, waits for them, and re-layouts  1.67 us (6%)
    pallas_call x1, Pallas kernels, in_one_kernel(): pl.pallas_call(functools.partial(kernel, plan), out_shape=jax.ShapeDtypeS...  26 us
    unnamed x1, local copies, waits for them, and re-layouts  1.67 us

profile of v2, /device:TPU:0, one launch (start us, length us, event | category | flops | bytes accessed | tf_op | source)
XLA Modules:
  0.0 27.7 jit_solution(1304647870948665020)
XLA Ops:
  0.0 26.0 %factor_solve.1 = f32[256,256]{1,0:T(8,128)} custom-call(bf16[3,512,256]{2,1,0:T(8,128)(2,1)} %bitcast.5, s32[3,512]{1,0:T(4,128)} %bitcast.6, s32[2,64]{1,0:T(2,128)} %bitcast.7, bf16[1728,256]{1,0:T(8,128)(2,1)} %bitcast.4), custom_call_target="tpu_custom_call" | custom-call | tf_op jit(solution)/shard_map/factor_solve/pallas_call | solution.py:281
  26.0 1.7 %copy.6 = f32[256,256]{1,0:T(8,128)} copy(f32[256,256]{1,0:T(8,128)} %factor_solve.1) | data formatting | bytes 524288

commit v3 on v2

--- a/solution.py
+++ b/solution.py
@@ -280,7 +280,7 @@
     anywhere = pl.BlockSpec(memory_space=pl.ANY)
     return pl.pallas_call(
         functools.partial(kernel, plan),
-        out_shape=jax.ShapeDtypeStruct((rows_dev, width), F32),
+        out_shape=pltpu.VMEM((rows_dev, width), F32),
         in_specs=[anywhere] * 4,
         out_specs=pl.BlockSpec(memory_space=pltpu.VMEM),
         scratch_shapes=[

time: 27.9 us -> 26.2 us (0.939)
  local copies, waits for them, and re-layouts: 1.67 us -> 0.71 us
  Pallas kernels: 26 us -> 25.3 us
    unnamed x1, local copies, waits for them, and re-layouts: 1.67 us -> 0.71 us
    pallas_call x1, Pallas kernels: 26 us -> 25.3 us  [in_one_kernel(): pl.pallas_call(functools.partial(kernel, plan), out_shape=pltpu.VMEM((row...]
where the time goes in v3:
time: 26.2 us; the launch traced here: 26 us
  Pallas kernels  25.3 us (97%)
  local copies, waits for them, and re-layouts  0.71 us (3%)
    pallas_call x1, Pallas kernels, in_one_kernel(): pl.pallas_call(functools.partial(kernel, plan), out_shape=pltpu.VMEM((row...  25.3 us
    unnamed x1, local copies, waits for them, and re-layouts  0.71 us

profile of v3, /device:TPU:0, one launch (start us, length us, event | category | flops | bytes accessed | tf_op | source)
XLA Modules:
  0.0 26.0 jit_solution(10393006127074458164)
XLA Ops:
  0.0 25.3 %factor_solve.1 = f32[256,256]{1,0:T(8,128)S(1)} custom-call(bf16[3,512,256]{2,1,0:T(8,128)(2,1)} %bitcast.5, s32[3,512]{1,0:T(4,128)} %bitcast.6, s32[2,64]{1,0:T(2,128)} %bitcast.7, bf16[1728,256]{1,0:T(8,128)(2,1)} %bitcast.4), custom_call_target="tpu_custom_call" | custom-call | tf_op jit(solution)/shard_map/factor_solve/pallas_call | solution.py:281
  25.3 0.7 %copy.6 = f32[256,256]{1,0:T(8,128)} copy(f32[256,256]{1,0:T(8,128)S(1)} %factor_solve.1) | data formatting | bytes 524288

commit v4 on v3

--- a/solution.py
+++ b/solution.py
@@ -97,7 +97,7 @@
     er_hbm, cor_hbm, sh_hbm, x_hbm,
     out_ref,
     er, cor, sh, xt,
-    halo_out, halo_in, own, rhs, part, l1_in, rs_in, ex_out, ex_in, final,
+    halo_out, halo_in, own, rhs, part, l1_in, rs_in, ex_out, ex_in, final, turned,
     in_sem, halo_s, halo_r, l1_s, l1_r, rs_s, rs_r, ex_s, ex_r, ag_s, ag_r,
 ):
     row, col = lax.axis_index("row"), lax.axis_index("col")
@@ -183,14 +183,19 @@
     received = jnp.concatenate([high, low], axis=0)
     assembled = own[...] + jnp.dot(share_map, received, preferred_element_type=F32)
     rhs[...] = assembled.astype(BF16)
-    part[...] = jnp.dot(xt[inner:, :], rhs[...], preferred_element_type=F32).reshape(part.shape)
+
+    def partial(low, high):
+        rows = xt[inner + plan.sep * (low - 1) : inner + plan.sep * high, :]
+        block = jnp.dot(rows, rhs[...], preferred_element_type=F32)
+        part[low - 1 : high] = block.reshape(high - low + 1, plan.sep, -1)
+
 
     def own_rows(level, ahead=0):
         span, rows = plan.span(level), plan.piece(level)
         return pl.ds(pl.multiple_of((col % span + ahead) % span * rows, 8), rows)
 
     rs, ex, ag = {}, {}, {}
-    for low, high in plan.groups:
+    def scatter(low, high):
         count = high - low + 1
         for m in range(1, plan.span(low)):
             rs[low, m] = remote(
@@ -200,11 +205,15 @@
                 rs_r.at[low - 1, m - 1],
                 col_peer(plan.span(low), m),
             )
-    first = remote(part.at[0], l1_in, l1_s.at[0], l1_r.at[0], col_peer(2, 1))
-    sent += list(rs.values()) + [first]
-
+    partial(*plan.groups[0])
+    scatter(*plan.groups[0])
+    partial(1, plan.col_bits)
     weights = jnp.dot(xt[:inner, :], rhs[...], preferred_element_type=F32).astype(BF16)
     out_ref[...] = tdot(xt[:inner, :], weights)
+    for group in plan.groups[1:]:
+        scatter(*group)
+    turned[...] = xt[inner:, :].T
+    sent += list(rs.values())
 
     def gather(low, high):
         count = high - low + 1
@@ -244,7 +253,8 @@
                         ex_r.at[at_level, k - 1],
                         row_peer(plan.row_span(level), k),
                     )
-    sent += list(ex.values())
+    first = remote(part.at[0], l1_in, l1_s.at[0], l1_r.at[0], col_peer(2, 1))
+    sent += list(ex.values()) + [first]
     if plan.levels > plan.col_bits:
         low, high = plan.groups[0]
         for level in range(low, high + 1):
@@ -254,14 +264,23 @@
                 ex[level, k].wait_recv()
                 total = total + ex_in[at_level, k - 1]
             final[level - 1, own_rows(level)] = total
-        gather(low, high)
+            gather(level, level)
     sent += list(ag.values())
+
+    def applied(low, high):
+        coef = final[low - 1 : high].reshape(plan.sep * (high - low + 1), -1).astype(BF16)
+        return jnp.dot(turned[:, plan.sep * (low - 1) : plan.sep * high], coef, preferred_element_type=F32)
+
     first.wait_recv()
     final[0] = part[0] + l1_in[...]
-    for copy in ag.values():
-        copy.wait_recv()
-    coef = final[...].reshape(plan.sep * levels, -1).astype(BF16)
-    out_ref[...] += tdot(xt[inner:, :], coef)
+    for (low, m), copy in ag.items():
+        if low < plan.groups[0][0]:
+            copy.wait_recv()
+    out_ref[...] += applied(1, plan.col_bits)
+    for (low, m), copy in ag.items():
+        if low >= plan.groups[0][0]:
+            copy.wait_recv()
+    out_ref[...] += applied(*plan.groups[0])
     for copy in sent:
         copy.wait_send()
 
@@ -298,6 +317,7 @@
             pltpu.VMEM((row_levels, small, width), F32),
             pltpu.VMEM((row_levels, row_slots, small, width), F32),
             pltpu.VMEM((levels, sep, width), F32),
+            pltpu.VMEM((rows_dev, sep * levels), BF16),
             dma((4,)),
             dma((2,)),
             dma((2,)),

time: 26.2 us -> 25.9 us (0.989)
  Pallas kernels: 25.3 us -> 25 us
    pallas_call x1, Pallas kernels: 25.3 us -> 25 us  [in_one_kernel(): pl.pallas_call(functools.partial(kernel, plan), out_shape=pltpu.VMEM((row...]
where the time goes in v4:
time: 25.9 us; the launch traced here: 25.7 us
  Pallas kernels  25 us (97%)
  local copies, waits for them, and re-layouts  0.71 us (3%)
    pallas_call x1, Pallas kernels, in_one_kernel(): pl.pallas_call(functools.partial(kernel, plan), out_shape=pltpu.VMEM((row...  25 us
    unnamed x1, local copies, waits for them, and re-layouts  0.71 us

profile of v4, /device:TPU:0, one launch (start us, length us, event | category | flops | bytes accessed | tf_op | source)
XLA Modules:
  0.0 25.7 jit_solution(12805473261723605547)
XLA Ops:
  0.0 25.0 %factor_solve.1 = f32[256,256]{1,0:T(8,128)S(1)} custom-call(bf16[3,512,256]{2,1,0:T(8,128)(2,1)} %bitcast.5, s32[3,512]{1,0:T(4,128)} %bitcast.6, s32[2,64]{1,0:T(2,128)} %bitcast.7, bf16[1728,256]{1,0:T(8,128)(2,1)} %bitcast.4), custom_call_target="tpu_custom_call" | custom-call | tf_op jit(solution)/shard_map/factor_solve/pallas_call | solution.py:300
  25.0 0.7 %copy.6 = f32[256,256]{1,0:T(8,128)} copy(f32[256,256]{1,0:T(8,128)S(1)} %factor_solve.1) | data formatting | bytes 524288

commit v5 on v4

--- a/solution.py
+++ b/solution.py
@@ -71,7 +71,7 @@
         self.col_bits = n_col.bit_length() - 1
         self.groups = []
         if self.levels > self.col_bits:
-            self.groups.append((self.col_bits + 1, self.levels))
+            self.groups += [(level, level) for level in range(self.levels, self.col_bits, -1)]
         self.groups += [(level, level) for level in range(self.col_bits, 1, -1)]
 
     def span(self, level):
@@ -205,13 +205,16 @@
                 rs_r.at[low - 1, m - 1],
                 col_peer(plan.span(low), m),
             )
-    partial(*plan.groups[0])
-    scatter(*plan.groups[0])
+    partial(plan.col_bits + 1, levels)
+    for group in plan.groups:
+        if group[0] > plan.col_bits:
+            scatter(*group)
     partial(1, plan.col_bits)
     weights = jnp.dot(xt[:inner, :], rhs[...], preferred_element_type=F32).astype(BF16)
     out_ref[...] = tdot(xt[:inner, :], weights)
-    for group in plan.groups[1:]:
-        scatter(*group)
+    for group in plan.groups:
+        if group[0] <= plan.col_bits:
+            scatter(*group)
     turned[...] = xt[inner:, :].T
     sent += list(rs.values())
 
@@ -256,7 +259,7 @@
     first = remote(part.at[0], l1_in, l1_s.at[0], l1_r.at[0], col_peer(2, 1))
     sent += list(ex.values()) + [first]
     if plan.levels > plan.col_bits:
-        low, high = plan.groups[0]
+        low, high = plan.col_bits + 1, levels
         for level in range(low, high + 1):
             at_level = level - plan.col_bits - 1
             total = ex_out[at_level]
@@ -274,13 +277,13 @@
     first.wait_recv()
     final[0] = part[0] + l1_in[...]
     for (low, m), copy in ag.items():
-        if low < plan.groups[0][0]:
+        if low <= plan.col_bits:
             copy.wait_recv()
     out_ref[...] += applied(1, plan.col_bits)
     for (low, m), copy in ag.items():
-        if low >= plan.groups[0][0]:
+        if low > plan.col_bits:
             copy.wait_recv()
-    out_ref[...] += applied(*plan.groups[0])
+    out_ref[...] += applied(plan.col_bits + 1, levels)
     for copy in sent:
         copy.wait_send()
 

time: 25.9 us -> 25.7 us (level)
  no operation moved by 1% of the time
where the time goes in v5:
time: 25.7 us; the launch traced here: 25.5 us
  Pallas kernels  24.8 us (96%)
  local copies, waits for them, and re-layouts  0.71 us (3%)
    pallas_call x1, Pallas kernels, in_one_kernel(): pl.pallas_call(functools.partial(kernel, plan), out_shape=pltpu.VMEM((row...  24.8 us
    unnamed x1, local copies, waits for them, and re-layouts  0.71 us

profile of v5, /device:TPU:0, one launch (start us, length us, event | category | flops | bytes accessed | tf_op | source)
XLA Modules:
  0.0 25.5 jit_solution(12399524987916199416)
XLA Ops:
  0.0 24.8 %factor_solve.1 = f32[256,256]{1,0:T(8,128)S(1)} custom-call(bf16[3,512,256]{2,1,0:T(8,128)(2,1)} %bitcast.5, s32[3,512]{1,0:T(4,128)} %bitcast.6, s32[2,64]{1,0:T(2,128)} %bitcast.7, bf16[1728,256]{1,0:T(8,128)(2,1)} %bitcast.4), custom_call_target="tpu_custom_call" | custom-call | tf_op jit(solution)/shard_map/factor_solve/pallas_call | solution.py:303
  24.8 0.7 %copy.6 = f32[256,256]{1,0:T(8,128)} copy(f32[256,256]{1,0:T(8,128)S(1)} %factor_solve.1) | data formatting | bytes 524288

commit v6 on v5

--- a/solution.py
+++ b/solution.py
@@ -215,6 +215,7 @@
     for group in plan.groups:
         if group[0] <= plan.col_bits:
             scatter(*group)
+    first = remote(part.at[0], l1_in, l1_s.at[0], l1_r.at[0], col_peer(2, 1))
     turned[...] = xt[inner:, :].T
     sent += list(rs.values())
 
@@ -245,7 +246,7 @@
         if low <= plan.col_bits:
             gather(low, high)
             continue
-        for k in range(1, plan.n_row):
+        for k in range(plan.n_row - 1, 0, -1):
             for level in range(low, high + 1):
                 if k < plan.row_span(level):
                     at_level = level - plan.col_bits - 1
@@ -256,7 +257,6 @@
                         ex_r.at[at_level, k - 1],
                         row_peer(plan.row_span(level), k),
                     )
-    first = remote(part.at[0], l1_in, l1_s.at[0], l1_r.at[0], col_peer(2, 1))
     sent += list(ex.values()) + [first]
     if plan.levels > plan.col_bits:
         low, high = plan.col_bits + 1, levels

time: 25.7 us -> 25.7 us (level)
  no operation moved by 1% of the time
where the time goes in v6:
time: 25.7 us; the launch traced here: 25.5 us
  Pallas kernels  24.8 us (96%)
  local copies, waits for them, and re-layouts  0.71 us (3%)
    pallas_call x1, Pallas kernels, in_one_kernel(): pl.pallas_call(functools.partial(kernel, plan), out_shape=pltpu.VMEM((row...  24.8 us
    unnamed x1, local copies, waits for them, and re-layouts  0.71 us

profile of v6, /device:TPU:0, one launch (start us, length us, event | category | flops | bytes accessed | tf_op | source)
XLA Modules:
  0.0 25.5 jit_solution(7733410703422207159)
XLA Ops:
  0.0 24.8 %factor_solve.1 = f32[256,256]{1,0:T(8,128)S(1)} custom-call(bf16[3,512,256]{2,1,0:T(8,128)(2,1)} %bitcast.5, s32[3,512]{1,0:T(4,128)} %bitcast.6, s32[2,64]{1,0:T(2,128)} %bitcast.7, bf16[1728,256]{1,0:T(8,128)(2,1)} %bitcast.4), custom_call_target="tpu_custom_call" | custom-call | tf_op jit(solution)/shard_map/factor_solve/pallas_call | solution.py:303
  24.8 0.7 %copy.6 = f32[256,256]{1,0:T(8,128)} copy(f32[256,256]{1,0:T(8,128)S(1)} %factor_solve.1) | data formatting | bytes 524288
